TPU v7x, 32 devices: a whole 2x2x4 slice. The times are simulated.
32 devices in a mesh: dp: 4 (over z), tensor: 8 (over y, x, core).
Axes of the slice: x: 2, y: 2, z: 4, core: 2. Of those that a mesh axis runs over, the one named last changes fastest.
Arguments:
- teacher_hidden: bfloat16 [64, 5120], P('dp', 'tensor'), may hold values from -200 to 200
- student_hidden: bfloat16 [64, 4096], P('dp', 'tensor'), may hold values from -8 to 8
- teacher_head: bfloat16 [5120, 8192], P(None, ('dp', 'tensor')), may hold values from -6 to 6
- student_head: bfloat16 [4096, 8192], P(None, ('dp', 'tensor')), may hold values from -6 to 6
- teacher_gain: float32 [5120], replicated, may hold values from 0.5 to 1.5
- lengths: int32 [8], replicated, may hold values from 1 to 8, as said below
- student_row: int32 [64], replicated, may hold values from 0 to 63, as said below
- targets: int32 [64], replicated, may hold values from 0 to 8191
Outputs:
- grad_logits: bfloat16 [64, 8192], P(None, ('dp', 'tensor'))
- divergence: float32 [64], P('dp')
- log_ratio: float32 [64], P('dp')
Inputs may be any that keep to these rules, and one draw needn't show every extreme that they name: The lengths of the 2 responses of one index of dp sum to at most 8, and to exactly 8 on some index. `student_row`: a permutation: every row of student_hidden is named once.
All inputs are finite; a program needn't handle non-finite values.
Results may differ from a plain program's by a relative error of at most 0.01095.
Values may be sent and summed in bfloat16 or wider, within the bound.
A program may use at most 64 MiB of HBM per device.

v0:
```python
import jax
import jax.numpy as jnp
from jax import lax
from jax.sharding import PartitionSpec as P

SLOT = 8


def merged_2(array, axis, combine):
    everything = jax.tree.map(lambda part: lax.all_gather(part, axis), array)
    initial = jax.tree.map(lambda part: part[0], everything)

    def turn(k, so_far):
        return combine(so_far, jax.tree.map(lambda part: part[k], everything))

    return lax.fori_loop(1, lax.axis_size(axis), turn, initial)


def on_device(
    teacher_hidden,
    student_hidden,
    teacher_head,
    student_head,
    teacher_gain,
    lengths,
    student_row,
    targets,
):
    dp_count = lax.axis_size("dp")
    tensor_count = lax.axis_size("tensor")
    local_tokens = teacher_hidden.shape[0]
    token_count = local_tokens * dp_count
    vocab_local = teacher_head.shape[1]
    dp_index = lax.axis_index("dp")
    vocab_start = (dp_index * tensor_count + lax.axis_index("tensor")) * vocab_local
    token_ids = jnp.arange(token_count, dtype=jnp.int32)
    live_all = (token_ids % SLOT < lengths[token_ids // SLOT]).astype(jnp.float32)
    teacher_full, student_full = (
        lax.all_gather(teacher_hidden, "tensor", axis=1, tiled=True),
        lax.all_gather(student_hidden, "tensor", axis=1, tiled=True),
    )
    values = lax.all_gather(teacher_full, "dp", axis=0, tiled=True).astype(jnp.float32)
    row_scale = lax.rsqrt(jnp.mean(values * values, axis=1, keepdims=True) + 1e-06)
    normed = (values * row_scale * teacher_gain[None, :]).astype(jnp.bfloat16)
    teacher_logits = jnp.dot(normed, teacher_head, preferred_element_type=jnp.float32)
    student_all = lax.all_gather(student_full, "dp", axis=0, tiled=True)
    chosen_rows = student_all[student_row[token_ids]]
    student_logits = jnp.dot(chosen_rows, student_head, preferred_element_type=jnp.float32)
    target_local = targets[token_ids] - vocab_start
    target_hits = (
        target_local[:, None] == jnp.arange(vocab_local, dtype=jnp.int32)[None, :]
    ).astype(jnp.float32)
    target_teacher = jnp.sum(target_hits * teacher_logits, axis=1)
    target_student = jnp.sum(target_hits * student_logits, axis=1)
    teacher_max = jnp.max(teacher_logits, axis=1)
    student_max = jnp.max(student_logits, axis=1)
    teacher_exp = jnp.exp(teacher_logits - teacher_max[:, None])
    student_exp = jnp.exp(student_logits - student_max[:, None])
    cross_sum = jnp.sum(student_exp * (student_logits - teacher_logits), axis=1)

    def combine(earlier, later):
        top_teacher = jnp.maximum(earlier[0], later[0])
        teacher_total = earlier[1] * jnp.exp(earlier[0] - top_teacher) + later[1] * jnp.exp(
            later[0] - top_teacher
        )
        top_student = jnp.maximum(earlier[2], later[2])
        early_rescale = jnp.exp(earlier[2] - top_student)
        late_rescale = jnp.exp(later[2] - top_student)
        return (
            top_teacher,
            teacher_total,
            top_student,
            earlier[3] * early_rescale + later[3] * late_rescale,
            earlier[4] * early_rescale + later[4] * late_rescale,
            earlier[5] + later[5],
            earlier[6] + later[6],
        )

    merged = merged_2(
        (
            teacher_max,
            jnp.sum(teacher_exp, axis=1),
            student_max,
            jnp.sum(student_exp, axis=1),
            cross_sum,
            target_teacher,
            target_student,
        ),
        ("dp", "tensor"),
        combine,
    )
    teacher_lse = merged[0] + jnp.log(merged[1])
    student_lse = merged[2] + jnp.log(merged[3])
    teacher_logp = teacher_logits - teacher_lse[:, None]
    student_logp = student_logits - student_lse[:, None]
    student_prob = jnp.exp(student_logp)
    kl_raw = merged[4] / merged[3] - student_lse + teacher_lse
    picked_teacher = merged[5]
    picked_student = merged[6]
    gradient = (
        live_all[:, None] * student_prob * (student_logp - teacher_logp - kl_raw[:, None])
    ).astype(jnp.bfloat16)
    kl_rows = live_all * kl_raw
    ratio_rows = live_all * (picked_student - student_lse - (picked_teacher - teacher_lse))
    divergence = lax.dynamic_slice_in_dim(kl_rows, dp_index * local_tokens, local_tokens)
    log_ratio = lax.dynamic_slice_in_dim(ratio_rows, dp_index * local_tokens, local_tokens)
    return (gradient, divergence, log_ratio)


def solution(mesh):
    return jax.shard_map(
        on_device,
        mesh=mesh,
        in_specs=(
            P("dp", "tensor"),
            P("dp", "tensor"),
            P(None, ("dp", "tensor")),
            P(None, ("dp", "tensor")),
            P(),
            P(),
            P(),
            P(),
        ),
        out_specs=(P(None, ("dp", "tensor")), P("dp"), P("dp")),
        check_vma=False,
    )
```

profile of v0, /device:TPU:0, one launch (start us, length us, event | category | flops | bytes accessed | tf_op | source)
XLA Modules:
  0.0 115.9 jit_solution(16936663235237315496)
XLA Ops:
  0.7 1.6 %gather_fusion.2 = s32[64]{0:T(128)S(1)} fusion(s32[64]{0:T(128)} %param.17, s32[1024]{0:T(1024)S(1)} %pad_clamp_fusion.1), kind=kCustom, calls=%fused_computation.2 | custom fusion | bytes 768 | tf_op jit(solution)/shard_map/gather | solution.py:49
  2.3 11.0 %all_gather.56 = bf16[16,5120]{1,0:T(8,128)(2,1)S(1)} all-gather(bf16[16,640]{1,0:T(8,128)(2,1)} %param.10), channel_id=1, replica_groups=mesh['dp'=4,'tensor'=8] {'tensor'}, dimensions={1}, use_global_device_ids=true | all-gather | bytes 184320 | tf_op jit(solution)/shard_map/all_gather | solution.py:39
  13.2 18.4 %all_gather.57 = bf16[64,5120]{1,0:T(8,128)(2,1)S(1)} all-gather(bf16[16,5120]{1,0:T(8,128)(2,1)S(1)} %all_gather.56), channel_id=1, replica_groups=mesh['dp'=4,'tensor'=8] {'dp'}, dimensions={0}, use_global_device_ids=true | all-gather | bytes 819200 | tf_op jit(solution)/shard_map/all_gather | solution.py:42
  31.6 0.2 fusion.17
  31.9 0.7 fusion.32
  32.6 0.8 gather_fusion
  33.4 9.0 %all_gather.54 = bf16[16,4096]{1,0:T(8,128)(2,1)S(1)} all-gather(bf16[16,512]{1,0:T(8,128)(2,1)S(1)} %copy-done.4), channel_id=1, replica_groups=mesh['dp'=4,'tensor'=8] {'tensor'}, dimensions={1}, use_global_device_ids=true | all-gather | bytes 147456 | tf_op jit(solution)/shard_map/all_gather | solution.py:40
  42.4 15.5 %all_gather.55 = bf16[64,4096]{1,0:T(8,128)(2,1)S(1)} all-gather(bf16[16,4096]{1,0:T(8,128)(2,1)S(1)} %all_gather.54), channel_id=1, replica_groups=mesh['dp'=4,'tensor'=8] {'dp'}, dimensions={0}, use_global_device_ids=true | all-gather | bytes 655360 | tf_op jit(solution)/shard_map/all_gather | solution.py:46
  57.9 1.7 %gather_fusion.1 = bf16[64,4096]{1,0:T(8,128)(2,1)} fusion(bf16[64,4096]{1,0:T(8,128)(2,1)S(1)} %all_gather.55, s32[1024]{0:T(1024)S(1)} %pad_clamp_fusion), kind=kCustom, calls=%fused_computation.1 | custom fusion | bytes 1048832 | tf_op jit(solution)/shard_map/gather | solution.py:47
  59.6 2.3 %fusion.33 = (f32[64]{0:T(128)S(1)}, f32[64,256]{1,0:T(8,128)S(1)}) fusion(bf16[64,4096]{1,0:T(8,128)(2,1)} %gather_fusion.1, bf16[4096,256]{1,0:T(8,128)(2,1)} %param.13), kind=kOutput, calls=%fused_computation.73 | convolution fusion | flops 134234048 | bytes 2687232 | tf_op jit(solution)/shard_map/dot_general | solution.py:48
  61.9 0.3 multiply_reduce_fusion
  62.2 0.3 dynamic-update-slice.3
  62.5 0.3 dynamic-update-slice.4
  62.8 0.3 dynamic-update-slice.5
  63.0 0.3 dynamic-update-slice.6
  63.3 0.3 dynamic-update-slice.1
  63.6 0.3 dynamic-update-slice
  63.8 0.3 dynamic-update-slice.2
  64.1 40.1 %all-reduce.7 = (f32[2048]{0:T(1024)S(1)}, f32[2048]{0:T(1024)S(1)}, f32[2048]{0:T(1024)S(1)}, f32[2048]{0:T(1024)S(1)}, f32[2048]{0:T(1024)S(1)}, /*index=5*/f32[2048]{0:T(1024)S(1)}, f32[2048]{0:T(1024)S(1)}) all-reduce(f32[2048]{0:T(1024)S(1)} %dynamic-update-slice, ...), channel_id=2, replica_groups=mesh['dp'=4,'tensor'=8] {'dp','tensor'}, use_global_device_ids=true, to_apply=%add | all-reduce | flops 14336 | bytes 114688
  104.2 0.1 reshape.131
  104.3 0.1 reshape.132
  104.3 0.1 reshape.133
  104.4 0.1 reshape.134
  104.5 0.1 reshape.135
  104.5 0.1 reshape.136
  104.6 0.1 reshape.137
  104.7 3.5 %while.27 = (s32[]{:T(128)}, f32[64]{0:T(128)S(1)}, f32[64]{0:T(128)S(1)}, f32[64]{0:T(128)S(1)}, f32[64]{0:T(128)S(1)}, /*index=5*/f32[64]{0:T(128)S(1)}, f32[6...) while((s32[]{:T(128)}, f32[64]{0:T(128)S(1)}, ...), condition=%wide.region_9.10_spmd, body=%wide.region_8.9_spmd.sunk | while | flops 1221 | bytes 6875 | solution.py:16
  108.2 0.7 fusion.31
  108.9 5.1 %subtract_select_fusion = (f32[64]{0:T(128)S(1)}, pred[64]{0:T(512)(128)(4,1)S(1)}, f32[64]{0:T(128)S(1)}, f32[64]{0:T(128)S(1)}) fusion(f32[64]{0:T(128)S(1)} %get-tuple-element.367, f32[64]{0:T(128)S(1)} %get-tuple-element.366, s32[]{:T(128)} %bitcast.15, s32[]{:T(128)} %bitcast.14, s32[]{:T(128)} %bitcast.13, s32[]{:T(128)} %bitcast.12, s32[]{:T(128)} %bitcast.11, ...), kind=kLoop, calls=%fused_computation.64 | loop fusion | flops 2432 | bytes 2400 | tf_op jit(solution)/shard_map/mul | solution.py:104
  114.0 0.7 multiply_convert_fusion
  114.7 0.6 dynamic_slice.76
  115.3 0.6 dynamic_slice.77
  (156 shorter events, 2.5 us)
Async XLA Ops:
  0.6 31.2 %copy-start = (bf16[5120,256]{1,0:T(8,128)(2,1)S(1)}, bf16[5120,256]{1,0:T(8,128)(2,1)}, u32[]{:S(2)}) copy-start(bf16[5120,256]{1,0:T(8,128)(2,1)} %param.12) | copy-start | bytes 7864324
  0.6 31.2 %copy-start.3 = (f32[5120]{0:T(1024)S(1)}, f32[5120]{0:T(1024)}, u32[]{:S(2)}) copy-start(f32[5120]{0:T(1024)} %param.14) | copy-start | bytes 61444
  31.6 1.0 copy-start.1
  31.8 1.6 %copy-start.4 = (bf16[16,512]{1,0:T(8,128)(2,1)S(1)}, bf16[16,512]{1,0:T(8,128)(2,1)}, u32[]{:S(2)}) copy-start(bf16[16,512]{1,0:T(8,128)(2,1)} %param.11) | copy-start | bytes 49156
  59.6 48.6 %copy-start.2 = (s32[8]{0:T(128)S(1)}, s32[8]{0:T(128)}, u32[]{:S(2)}) copy-start(s32[8]{0:T(128)} %param.15) | copy-start | bytes 100
where the time goes:
time: 116 us
  blocking collectives  94 us (81%)
  other arithmetic  8.71 us (8%)
  local copies, waits for them, and re-layouts  8.31 us (7%)
  matrix products  3.05 us (3%)
    unnamed x1, blocking collectives  40.1 us
    all_gather x1, blocking collectives, on_device(): lax.all_gather(teacher_full, 'dp', axis=0, tiled=True).astype(jnp.float32)  18.4 us
    all_gather x1, blocking collectives, on_device(): student_all = lax.all_gather(student_full, 'dp', axis=0, tiled=True)  15.5 us
    all_gather x1, blocking collectives, on_device(): lax.all_gather(teacher_hidden, 'tensor', axis=1, tiled=True)  11 us
    all_gather x1, blocking collectives, on_device(): lax.all_gather(student_hidden, 'tensor', axis=1, tiled=True)  9.03 us
    mul x1, other arithmetic, on_device(): live_all * (picked_student - student_lse - (picked_teacher - teacher_lse))  5.07 us
    gather x2, local copies, waits for them, and re-layouts, on_device(): chosen_rows = student_all[student_row[token_ids]]  2.44 us
    dot_general x1, matrix products, on_device(): jnp.dot(chosen_rows, student_head, preferred_element_type=jnp.float32)  2.34 us

commit v1 on v0

--- a/solution.py
+++ b/solution.py
@@ -36,7 +36,7 @@
     token_ids = jnp.arange(token_count, dtype=jnp.int32)
     live_all = (token_ids % SLOT < lengths[token_ids // SLOT]).astype(jnp.float32)
     teacher_full, student_full = (
-        lax.all_gather(teacher_hidden, "tensor", axis=1, tiled=True),
+        jnp.concatenate(lax.all_gather(teacher_hidden, "tensor"), axis=1),
         lax.all_gather(student_hidden, "tensor", axis=1, tiled=True),
     )
     values = lax.all_gather(teacher_full, "dp", axis=0, tiled=True).astype(jnp.float32)

time: 116 us -> 116 us (level)
  no operation moved by 1% of the time
where the time goes in v1:
time: 116 us
  blocking collectives  94 us (81%)
  other arithmetic  8.71 us (8%)
  local copies, waits for them, and re-layouts  8.33 us (7%)
  matrix products  3.05 us (3%)
    unnamed x1, blocking collectives  40.1 us
    all_gather x1, blocking collectives, on_device(): lax.all_gather(teacher_full, 'dp', axis=0, tiled=True).astype(jnp.float32)  18.4 us
    all_gather x1, blocking collectives, on_device(): student_all = lax.all_gather(student_full, 'dp', axis=0, tiled=True)  15.5 us
    all_gather x1, blocking collectives, on_device(): lax.all_gather(teacher_hidden, 'tensor')  10.9 us
    all_gather x1, blocking collectives, on_device(): lax.all_gather(student_hidden, 'tensor', axis=1, tiled=True)  9.03 us
    mul x1, other arithmetic, on_device(): live_all * (picked_student - student_lse - (picked_teacher - teacher_lse))  5.07 us
    gather x2, local copies, waits for them, and re-layouts, on_device(): chosen_rows = student_all[student_row[token_ids]]  2.44 us
    dot_general x1, matrix products, on_device(): jnp.dot(chosen_rows, student_head, preferred_element_type=jnp.float32)  2.34 us

profile of v1, /device:TPU:0, one launch (start us, length us, event | category | flops | bytes accessed | tf_op | source)
XLA Modules:
  0.0 115.9 jit_solution(2874300564983139461)
XLA Ops:
  0.7 1.6 %gather_fusion.2 = s32[64]{0:T(128)S(1)} fusion(s32[64]{0:T(128)} %param.17, s32[1024]{0:T(1024)S(1)} %pad_clamp_fusion.1), kind=kCustom, calls=%fused_computation.2 | custom fusion | bytes 768 | tf_op jit(solution)/shard_map/gather | solution.py:49
  2.3 10.9 %all-gather = bf16[128,640]{1,0:T(8,128)(2,1)S(1)} all-gather(bf16[16,640]{1,0:T(8,128)(2,1)} %param.10), channel_id=2, replica_groups=mesh['dp'=4,'tensor'=8] {'tensor'}, dimensions={0}, use_global_device_ids=true | all-gather | bytes 184320 | tf_op jit(solution)/shard_map/all_gather | solution.py:39
  13.2 18.4 %all_gather.61 = bf16[64,5120]{1,0:T(8,128)(2,1)S(1)} all-gather(bf16[16,5120]{1,0:T(8,128)(2,1)S(1)} %bitcast.82), channel_id=1, replica_groups=mesh['dp'=4,'tensor'=8] {'dp'}, dimensions={0}, use_global_device_ids=true | all-gather | bytes 819200 | tf_op jit(solution)/shard_map/all_gather | solution.py:42
  31.6 0.2 fusion.17
  31.9 0.7 fusion.32
  32.6 0.8 gather_fusion
  33.4 9.0 %all_gather.57 = bf16[16,4096]{1,0:T(8,128)(2,1)S(1)} all-gather(bf16[16,512]{1,0:T(8,128)(2,1)S(1)} %copy-done.4), channel_id=1, replica_groups=mesh['dp'=4,'tensor'=8] {'tensor'}, dimensions={1}, use_global_device_ids=true | all-gather | bytes 147456 | tf_op jit(solution)/shard_map/all_gather | solution.py:40
  42.4 15.5 %all_gather.58 = bf16[64,4096]{1,0:T(8,128)(2,1)S(1)} all-gather(bf16[16,4096]{1,0:T(8,128)(2,1)S(1)} %all_gather.57), channel_id=1, replica_groups=mesh['dp'=4,'tensor'=8] {'dp'}, dimensions={0}, use_global_device_ids=true | all-gather | bytes 655360 | tf_op jit(solution)/shard_map/all_gather | solution.py:46
  57.9 1.7 %gather_fusion.1 = bf16[64,4096]{1,0:T(8,128)(2,1)} fusion(bf16[64,4096]{1,0:T(8,128)(2,1)S(1)} %all_gather.58, s32[1024]{0:T(1024)S(1)} %pad_clamp_fusion), kind=kCustom, calls=%fused_computation.1 | custom fusion | bytes 1048832 | tf_op jit(solution)/shard_map/gather | solution.py:47
  59.6 2.3 %fusion.33 = (f32[64]{0:T(128)S(1)}, f32[64,256]{1,0:T(8,128)S(1)}) fusion(bf16[64,4096]{1,0:T(8,128)(2,1)} %gather_fusion.1, bf16[4096,256]{1,0:T(8,128)(2,1)} %param.13), kind=kOutput, calls=%fused_computation.73 | convolution fusion | flops 134234048 | bytes 2687232 | tf_op jit(solution)/shard_map/dot_general | solution.py:48
  62.0 0.3 multiply_reduce_fusion
  62.3 0.3 dynamic-update-slice.3
  62.5 0.3 dynamic-update-slice.4
  62.8 0.3 dynamic-update-slice.5
  63.1 0.3 dynamic-update-slice.6
  63.3 0.3 dynamic-update-slice.1
  63.6 0.3 dynamic-update-slice
  63.8 0.3 dynamic-update-slice.2
  64.1 40.1 %all-reduce.7 = (f32[2048]{0:T(1024)S(1)}, f32[2048]{0:T(1024)S(1)}, f32[2048]{0:T(1024)S(1)}, f32[2048]{0:T(1024)S(1)}, f32[2048]{0:T(1024)S(1)}, /*index=5*/f32[2048]{0:T(1024)S(1)}, f32[2048]{0:T(1024)S(1)}) all-reduce(f32[2048]{0:T(1024)S(1)} %dynamic-update-slice, ...), channel_id=3, replica_groups=mesh['dp'=4,'tensor'=8] {'dp','tensor'}, use_global_device_ids=true, to_apply=%add | all-reduce | flops 14336 | bytes 114688
  104.2 0.1 reshape.140
  104.3 0.1 reshape.141
  104.3 0.1 reshape.142
  104.4 0.1 reshape.143
  104.5 0.1 reshape.144
  104.6 0.1 reshape.145
  104.6 0.1 reshape.146
  104.8 3.5 %while.27 = (s32[]{:T(128)}, f32[64]{0:T(128)S(1)}, f32[64]{0:T(128)S(1)}, f32[64]{0:T(128)S(1)}, f32[64]{0:T(128)S(1)}, /*index=5*/f32[64]{0:T(128)S(1)}, f32[6...) while((s32[]{:T(128)}, f32[64]{0:T(128)S(1)}, ...), condition=%wide.region_9.10_spmd, body=%wide.region_8.9_spmd.sunk | while | flops 1221 | bytes 6875 | solution.py:16
  108.2 0.7 fusion.31
  108.9 5.1 %subtract_select_fusion = (f32[64]{0:T(128)S(1)}, pred[64]{0:T(512)(128)(4,1)S(1)}, f32[64]{0:T(128)S(1)}, f32[64]{0:T(128)S(1)}) fusion(f32[64]{0:T(128)S(1)} %get-tuple-element.367, f32[64]{0:T(128)S(1)} %get-tuple-element.366, s32[]{:T(128)} %bitcast.15, s32[]{:T(128)} %bitcast.14, s32[]{:T(128)} %bitcast.13, s32[]{:T(128)} %bitcast.12, s32[]{:T(128)} %bitcast.11, ...), kind=kLoop, calls=%fused_computation.64 | loop fusion | flops 2432 | bytes 2400 | tf_op jit(solution)/shard_map/mul | solution.py:104
  114.0 0.7 multiply_convert_fusion
  114.8 0.6 dynamic_slice.76
  115.3 0.6 dynamic_slice.77
  (157 shorter events, 2.6 us)
Async XLA Ops:
  0.6 31.2 %copy-start = (bf16[5120,256]{1,0:T(8,128)(2,1)S(1)}, bf16[5120,256]{1,0:T(8,128)(2,1)}, u32[]{:S(2)}) copy-start(bf16[5120,256]{1,0:T(8,128)(2,1)} %param.12) | copy-start | bytes 7864324
  0.6 31.2 %copy-start.3 = (f32[5120]{0:T(1024)S(1)}, f32[5120]{0:T(1024)}, u32[]{:S(2)}) copy-start(f32[5120]{0:T(1024)} %param.14) | copy-start | bytes 61444
  31.6 1.0 copy-start.1
  31.9 1.6 %copy-start.4 = (bf16[16,512]{1,0:T(8,128)(2,1)S(1)}, bf16[16,512]{1,0:T(8,128)(2,1)}, u32[]{:S(2)}) copy-start(bf16[16,512]{1,0:T(8,128)(2,1)} %param.11) | copy-start | bytes 49156
  59.6 48.6 %copy-start.2 = (s32[8]{0:T(128)S(1)}, s32[8]{0:T(128)}, u32[]{:S(2)}) copy-start(s32[8]{0:T(128)} %param.15) | copy-start | bytes 100
